TPU v7x, 32 devices: a whole 2x2x4 slice. The times are simulated.
32 devices in a mesh: groups: 2 (over y), seq: 16 (over z, x, core).
Axes of the slice: x: 2, y: 2, z: 4, core: 2. Of those that a mesh axis runs over, the one named last changes fastest.
Arguments:
- token_ids: int32 [4096], P('groups'), parts along dimension 0, may hold values from 0 to 511
- vocab_table: bfloat16 [512, 3, 4096], P(None, None, 'seq'), may hold values from -6 to 6
- short_filter: float32 [7, 3, 4096], replicated, may hold values from -2 to 2
- residue: float32 [4096, 16], replicated, may hold values from -1.5 to 1.5
- decay: float32 [4096, 16], replicated, may hold values from 0.2 to 64
- skip_gain: float32 [4096], replicated, may hold values from -3 to 3
Outputs:
- hyena_out: bfloat16 [4096, 4096], P(('groups', 'seq')), parts along dimension 0
There are 2 independent parts, one for each index of `groups`. A program takes and returns all parts, laid end to end along the dimension named above; an argument that names none is the same for every part. Nothing has to cross between parts.
All inputs are finite; a program needn't handle non-finite values.
Results may differ from a plain program's by a relative error of at most 0.012.
Values may be sent and summed in bfloat16 or wider, within the bound.
A program may use at most 192 MiB of HBM per device.

v0:
```python
import functools
import math

import jax
import jax.numpy as jnp
from jax import lax
from jax.experimental import pallas as pl
from jax.experimental.pallas import tpu as pltpu
from jax.sharding import PartitionSpec as P

HIGHEST = lax.Precision.HIGHEST


def angle_tables(first_index, second_index, modulus):
    product = first_index[:, None] * second_index[None, :] % modulus
    angle = product.astype(jnp.float32) * (2.0 * math.pi / modulus)
    return (jnp.cos(angle), jnp.sin(angle))


def short_conv(padded, taps, count):
    width = taps.shape[0]
    total = jnp.zeros((count,) + padded.shape[1:], jnp.float32)
    for lag in range(width):
        start = width - 1 - lag
        total = total + taps[lag] * padded[start : start + count].astype(jnp.float32)
    return total


def filter_spectrum(freq, total, pole, gap, tail, scale):
    theta = freq.astype(jnp.float32) * (2.0 * math.pi / total)
    sine = jnp.sin(theta)[:, :, None, None]
    halfsq = (jnp.sin(0.5 * theta) ** 2)[:, :, None, None]
    parity = (1 - 2 * (freq % 2)).astype(jnp.float32)[:, :, None, None]
    shape_out = freq.shape + (pole.shape[0],)
    real_part = jnp.zeros(shape_out, jnp.float32)
    imag_part = jnp.zeros(shape_out, jnp.float32)
    for first in range(0, pole.shape[1], 4):
        part_pole = pole[:, first : first + 4]
        dreal = gap[:, first : first + 4] + 2.0 * part_pole * halfsq
        dimag = part_pole * sine
        factor = (
            scale[:, first : first + 4]
            * (1.0 - tail[:, first : first + 4] * parity)
            / (dreal * dreal + dimag * dimag)
        )
        real_part = real_part + jnp.sum(factor * dreal, axis=-1)
        imag_part = imag_part - jnp.sum(factor * dimag, axis=-1)
    return (real_part, imag_part)


def convolve(gated, skip, filters, total, move_forward, move_back):
    pieces, block, width = gated.shape
    span = 2 * pieces
    outer_index = jnp.arange(span, dtype=jnp.int32)
    piece_index = jnp.arange(pieces, dtype=jnp.int32)
    outer_cos, outer_sin = angle_tables(outer_index, piece_index, span)
    real_part = jnp.einsum("kp,ptc->ktc", outer_cos, gated, precision=HIGHEST)
    imag_part = -jnp.einsum("kp,ptc->ktc", outer_sin, gated, precision=HIGHEST)
    times = jnp.arange(block, dtype=jnp.int32)
    twist_cos, twist_sin = angle_tables(outer_index, times, total)
    twist_cos = twist_cos[:, :, None]
    twist_sin = twist_sin[:, :, None]
    turned_real = twist_cos * real_part + twist_sin * imag_part
    turned_imag = twist_cos * imag_part - twist_sin * real_part
    moved = move_forward(jnp.stack([turned_real, turned_imag]))
    count = moved.shape[1]
    length = moved.shape[2]
    positions = jnp.arange(length, dtype=jnp.int32)
    inner_cos, inner_sin = angle_tables(positions, positions, length)
    freq_real = jnp.einsum("mt,ktc->kmc", inner_cos, moved[0], precision=HIGHEST) + jnp.einsum(
        "mt,ktc->kmc", inner_sin, moved[1], precision=HIGHEST
    )
    freq_imag = jnp.einsum("mt,ktc->kmc", inner_cos, moved[1], precision=HIGHEST) - jnp.einsum(
        "mt,ktc->kmc", inner_sin, moved[0], precision=HIGHEST
    )
    owned = jnp.arange(count, dtype=jnp.int32)
    freq = (owned[:, None] + span * positions[None, :]) % total
    filt_real, filt_imag = filter_spectrum(freq, total, *filters)
    prod_real = freq_real * filt_real - freq_imag * filt_imag
    prod_imag = freq_real * filt_imag + freq_imag * filt_real
    back_real = jnp.einsum("mt,kmc->ktc", inner_cos, prod_real, precision=HIGHEST) - jnp.einsum(
        "mt,kmc->ktc", inner_sin, prod_imag, precision=HIGHEST
    )
    back_imag = jnp.einsum("mt,kmc->ktc", inner_cos, prod_imag, precision=HIGHEST) + jnp.einsum(
        "mt,kmc->ktc", inner_sin, prod_real, precision=HIGHEST
    )
    undo_cos, undo_sin = angle_tables(owned, positions, total)
    undo_cos = undo_cos[:, :, None]
    undo_sin = undo_sin[:, :, None]
    untwist_real = undo_cos * back_real - undo_sin * back_imag
    untwist_imag = undo_cos * back_imag + undo_sin * back_real
    returned = move_back(jnp.stack([untwist_real, untwist_imag]))
    last_cos, last_sin = angle_tables(piece_index, outer_index, span)
    convolved = (
        jnp.einsum("pk,ktc->ptc", last_cos, returned[0], precision=HIGHEST)
        - jnp.einsum("pk,ktc->ptc", last_sin, returned[1], precision=HIGHEST)
    ) * (1.0 / total)
    return convolved + skip * gated


def unchanged(value):
    return value


def body(token_ids, vocab_table, short_filter, residue, decay, skip_gain):
    pieces = lax.axis_size("seq")
    place = lax.axis_index("seq")
    length = token_ids.shape[0]
    local = length // pieces
    share = vocab_table.shape[2]
    rim = short_filter.shape[0] - 1
    total = 2 * length
    rate = decay / length
    pole = jnp.exp(-rate)
    gap = -jnp.expm1(-rate)
    tail = jnp.exp(-decay)
    scale = residue * jnp.sqrt(2.0 * rate)
    first_channel = place * share
    chan_taps = lax.dynamic_slice_in_dim(short_filter, first_channel, share, 2)
    chan_filters = (
        lax.dynamic_slice_in_dim(pole, first_channel, share, 0),
        lax.dynamic_slice_in_dim(gap, first_channel, share, 0),
        lax.dynamic_slice_in_dim(tail, first_channel, share, 0),
        lax.dynamic_slice_in_dim(scale, first_channel, share, 0),
    )
    chan_skip = lax.dynamic_slice_in_dim(skip_gain, first_channel, share, 0)
    streams = jnp.take(vocab_table, token_ids, axis=0)
    padded = jnp.pad(streams, ((rim, 0), (0, 0), (0, 0)))
    mixed = short_conv(padded, chan_taps, length)
    query = mixed[:, 0]
    gated = (mixed[:, 1] * mixed[:, 2]).reshape(pieces, local, share)
    convolved = convolve(gated, chan_skip, chan_filters, total, unchanged, unchanged)
    output = (query * convolved.reshape(length, share)).astype(jnp.bfloat16)
    return lax.all_to_all(output, "seq", split_axis=0, concat_axis=1, tiled=True)


LANES = 128
SUB = 8
HALO = 8
UNROLL = 8
CUTS = 4
SPLITS = 1
MESH = pl.DeviceIdType.MESH


def wide(row):
    return jnp.broadcast_to(row, (SUB, LANES))


def toggles(value, limit):
    steps, bit = [], 1
    while bit < limit:
        steps.append((bit, bit - 2 * bit * (value // bit % 2)))
        bit = 2 * bit
    return steps


def flip(value, steps, mask):
    for bit, step in steps:
        if mask & bit:
            value = value + step
    return value


def scan_kernel(
    pieces,
    local,
    width,
    modes,
    ids_ref,
    all_tab_ref,
    all_taps_ref,
    all_decay_ref,
    all_residue_ref,
    all_skip_ref,
    out_ref,
    tab_ref,
    taps_ref,
    decay_ref,
    residue_ref,
    skip_ref,
    load_sem,
    hot_ref,
    x_ref,
    query_ref,
    gated_ref,
    end_ref,
    begin_ref,
    coef_ref,
    turn_ref,
    send_ref,
    send_sem,
    recv_sem,
    own_sem,
):
    me = lax.axis_index("seq")
    slots = pieces // SUB
    steps = toggles(me, pieces)
    share = skip_ref.shape[1]
    vocab = tab_ref.shape[1]
    blocks = share // LANES
    length = pieces * local
    mine = pl.ds(pl.multiple_of(me * share, LANES), share)
    loads = (
        (all_tab_ref, tab_ref),
        (all_taps_ref.at[:, :, mine], taps_ref),
        (all_decay_ref.at[:, mine], decay_ref),
        (all_residue_ref.at[:, mine], residue_ref),
        (all_skip_ref.at[:, mine], skip_ref),
    )
    loads = [
        pltpu.make_async_copy(source, target, load_sem.at[i])
        for i, (source, target) in enumerate(loads)
    ]
    for load in loads:
        load.start()
    barrier = pltpu.get_barrier_semaphore()
    for mask in range(1, pieces):
        peer = flip(me, steps, mask)
        pl.semaphore_signal(barrier, inc=1, device_id={"seq": peer}, device_id_type=MESH)

    cut = (HALO + local) * pieces // CUTS
    ids = ids_ref[...]
    before = jnp.where(
        lax.broadcasted_iota(jnp.int32, ids.shape, 0) == 0, -1, pltpu.roll(ids, 1, axis=0)
    )
    entry = lax.broadcasted_iota(jnp.int32, (pieces, vocab), 1)
    count = (HALO + local) // CUTS

    def build(i):
        for t in range(i * count - HALO, (i + 1) * count - HALO):
            column = ids[:, t : t + 1] if t >= 0 else before[:, local + t : local + t + 1]
            hot_ref[(HALO + t) * pieces : (HALO + t + 1) * pieces, :] = jnp.where(
                column == entry, 1.0, 0.0
            ).astype(jnp.bfloat16)

    build(0)
    for load in loads:
        load.wait()

    height = local // SPLITS

    def place(block, part, source):
        return out_ref.at[
            pl.ds(part * height, height),
            pl.ds(pl.multiple_of(source * share + block * LANES, LANES), LANES),
        ]

    def remote(block, part, mask, peer, source):
        return pltpu.make_async_remote_copy(
            src_ref=send_ref.at[block, peer, pl.ds(part * height, height)],
            dst_ref=place(block, part, source),
            send_sem=send_sem.at[block, part, mask],
            recv_sem=recv_sem.at[block, part, mask],
            device_id={"seq": peer},
            device_id_type=MESH,
        )

    def own(block, part):
        return pltpu.make_async_copy(
            send_ref.at[block, me, pl.ds(part * height, height)],
            place(block, part, me),
            own_sem.at[block, part],
        )

    for block in range(blocks):
        lane = pl.ds(block * LANES, LANES)
        rate = decay_ref[:, lane] / length
        pole = jnp.exp(-rate)
        leap = jnp.exp(-rate * local)
        coef_ref[0] = pole
        coef_ref[1] = residue_ref[:, lane] * jnp.sqrt(2.0 * rate)
        skip = wide(skip_ref[:, lane])
        table = jnp.concatenate([tab_ref[j, :, lane] for j in range(3)], axis=1)
        for i in range(CUTS):
            if block == 0 and i + 1 < CUTS:
                build(i + 1)
            span = pl.ds(i * cut, cut)
            x_ref[span, :] = jnp.dot(hot_ref[span, :], table, preferred_element_type=jnp.float32)

        def first_pass(slot, _):
            base = pl.multiple_of(slot * SUB, SUB)
            poles = [wide(coef_ref[0, s : s + 1, :]) for s in range(modes)]
            taps = [
                [wide(taps_ref[j, lag : lag + 1, lane]) for lag in range(width)] for j in range(3)
            ]

            def step(i, state):
                state = list(state)
                mixed = []
                for j in range(3):
                    seen = {}
                    for t in range(1 - width, UNROLL):
                        at = pl.multiple_of((i * UNROLL + t + HALO) * pieces + base, SUB)
                        seen[t] = x_ref[pl.ds(at, SUB), j * LANES : (j + 1) * LANES]
                    totals = []
                    for t in range(UNROLL):
                        total = taps[j][0] * seen[t]
                        for lag in range(1, width):
                            total = total + taps[j][lag] * seen[t - lag]
                        totals.append(total)
                    mixed.append(totals)
                for t in range(UNROLL):
                    at = pl.multiple_of((i * UNROLL + t) * pieces + base, SUB)
                    gated = mixed[1][t] * mixed[2][t]
                    query_ref[pl.ds(at, SUB), :] = mixed[0][t]
                    gated_ref[pl.ds(at, SUB), :] = gated
                    for s in range(modes):
                        state[s] = poles[s] * state[s] + gated
                return tuple(state)

            zero = jnp.zeros((SUB, LANES), jnp.float32)
            state = lax.fori_loop(0, local // UNROLL, step, (zero,) * modes)
            for s in range(modes):
                end_ref[pl.ds(pl.multiple_of(s * pieces + base, SUB), SUB), :] = state[s]
            return 0

        lax.fori_loop(0, slots, first_pass, 0)
        carry = jnp.zeros((modes, LANES), jnp.float32)
        for k in range(pieces):
            begin_ref[pl.ds(k, modes, stride=pieces), :] = carry
            carry = leap * carry + end_ref[pl.ds(k, modes, stride=pieces), :]

        for far in range(slots - 1, -1, -1):
            first = flip(me // SUB * SUB, steps, far * SUB)
            base = pl.multiple_of(first, SUB)
            poles = [wide(coef_ref[0, s : s + 1, :]) for s in range(modes)]
            coefs = [wide(coef_ref[1, s : s + 1, :]) for s in range(modes)]

            def step(i, state):
                state = list(state)
                for t in range(UNROLL):
                    at = pl.multiple_of((i * UNROLL + t) * pieces + base, SUB)
                    gated = gated_ref[pl.ds(at, SUB), :]
                    terms = [skip * gated]
                    for s in range(modes):
                        state[s] = poles[s] * state[s] + gated
                        terms.append(coefs[s] * state[s])
                        if len(terms) == 5:
                            terms = [((terms[0] + terms[1]) + (terms[2] + terms[3])) + terms[4]]
                    total = terms[0]
                    for term in terms[1:]:
                        total = total + term
                    turn_ref[pl.ds(pl.multiple_of((i * UNROLL + t) * SUB, SUB), SUB), :] = (
                        query_ref[pl.ds(at, SUB), :] * total
                    )
                return tuple(state)

            state = tuple(
                begin_ref[pl.ds(pl.multiple_of(s * pieces + base, SUB), SUB), :]
                for s in range(modes)
            )
            for part in range(SPLITS):
                low = part * height
                state = lax.fori_loop(low // UNROLL, (low + height) // UNROLL, step, state)
                for k in range(SUB):
                    send_ref[block, first + k, low : low + height, :] = turn_ref[
                        pl.ds(low * SUB + k, height, stride=SUB), :
                    ].astype(jnp.bfloat16)
                if block == 0 and far == slots - 1 and part == 0:
                    pl.semaphore_wait(barrier, pieces - 1)
                for k in range(SUB):
                    if far == 0 and k == 0:
                        own(block, part).start()
                    else:
                        mask = far * SUB + k
                        remote(block, part, mask, flip(me, steps, mask), me).start()

    for block in range(blocks):
        for part in range(SPLITS):
            own(block, part).wait()
            for mask in range(1, pieces):
                peer = flip(me, steps, mask)
                remote(block, part, mask, peer, me).wait_send()
                remote(block, part, mask, me, peer).wait_recv()


def scan_body(token_ids, vocab_table, short_filter, residue, decay, skip_gain):
    pieces = lax.axis_size("seq")
    length = token_ids.shape[0]
    local = length // pieces
    vocab, streams, share = vocab_table.shape
    width = short_filter.shape[0]
    modes = decay.shape[1]
    blocks = share // LANES
    ids = token_ids.reshape(pieces, local)
    table = vocab_table.transpose(1, 0, 2)
    taps = short_filter.transpose(1, 0, 2)
    rows = (HALO + local) * pieces
    vmem = pl.BlockSpec(memory_space=pltpu.VMEM)
    return pl.pallas_call(
        functools.partial(scan_kernel, pieces, local, width, modes),
        out_shape=pltpu.VMEM((local, pieces * share), jnp.bfloat16),
        in_specs=[vmem] + [pl.BlockSpec(memory_space=pl.ANY)] * 5,
        out_specs=pl.BlockSpec(memory_space=pltpu.VMEM),
        scratch_shapes=[
            pltpu.VMEM((streams, vocab, share), vocab_table.dtype),
            pltpu.VMEM((streams, width, share), jnp.float32),
            pltpu.VMEM((modes, share), jnp.float32),
            pltpu.VMEM((modes, share), jnp.float32),
            pltpu.VMEM((1, share), jnp.float32),
            pltpu.SemaphoreType.DMA((5,)),
            pltpu.VMEM((rows, vocab), jnp.bfloat16),
            pltpu.VMEM((rows, streams * LANES), jnp.float32),
            pltpu.VMEM((length, LANES), jnp.float32),
            pltpu.VMEM((length, LANES), jnp.float32),
            pltpu.VMEM((modes * pieces, LANES), jnp.float32),
            pltpu.VMEM((modes * pieces, LANES), jnp.float32),
            pltpu.VMEM((2, modes, LANES), jnp.float32),
            pltpu.VMEM((local * SUB, LANES), jnp.float32),
            pltpu.VMEM((blocks, pieces, local, LANES), jnp.bfloat16),
            pltpu.SemaphoreType.DMA((blocks, SPLITS, pieces)),
            pltpu.SemaphoreType.DMA((blocks, SPLITS, pieces)),
            pltpu.SemaphoreType.DMA((blocks, SPLITS)),
        ],
        compiler_params=pltpu.CompilerParams(collective_id=0, has_side_effects=True),
    )(ids, table, taps, decay.T, residue.T, skip_gain[None])


def fits(mesh, share, local, width):
    pieces = mesh.shape["seq"]
    even = pieces % (2 * SUB) == 0 and pieces & (pieces - 1) == 0
    return share % LANES == 0 and even and local % (16 * SPLITS) == 0 and width <= HALO + 1


def solution(mesh):
    placed = (P("groups"), P(None, None, "seq"), P(), P(), P(), P())

    def whole(token_ids, vocab_table, short_filter, residue, decay, skip_gain):
        pieces = mesh.shape["seq"]
        local = token_ids.shape[0] // (mesh.shape["groups"] * pieces)
        share = vocab_table.shape[2] // pieces
        chosen = scan_body if fits(mesh, share, local, short_filter.shape[0]) else body
        return jax.shard_map(
            chosen, mesh=mesh, in_specs=placed, out_specs=P(("groups", "seq"), None), check_vma=False
        )(token_ids, vocab_table, short_filter, residue, decay, skip_gain)

    return whole
```

profile of v0, /device:TPU:9, one launch (start us, length us, event | category | flops | bytes accessed | tf_op | source)
XLA Modules:
  0.0 34.8 jit_solution(14743482543433842465)
XLA Ops:
  0.0 33.9 %shard_map.64 = bf16[128,4096]{1,0:T(8,128)(2,1)S(1)} custom-call(s32[16,128]{1,0:T(8,128)} %bitcast.11, bf16[3,512,256]{2,1,0:T(8,128)(2,1)} %bitcast.6, f32[3,7,4096]{2,1,0:T(8,128)} %bitcast.7, f32[16,4096]{1,0:T(8,128)} %bitcast.8, f32[16,4096]{1,0:T(8,128)} %bitcast.9, f32[1,4096]{1,0:T(1,128)} %bitcast.10), custom_call_target="tpu_custom_call" | custom-call | tf_op jit(solution)/shard_map/pallas_call | solution.py:391
  33.9 1.0 %copy.8 = bf16[128,4096]{1,0:T(8,128)(2,1)} copy(bf16[128,4096]{1,0:T(8,128)(2,1)S(1)} %shard_map.64) | data formatting | bytes 2097152
where the time goes:
time: 35 us; the launch traced here: 34.8 us
  Pallas kernels  33.9 us (97%)
  local copies, waits for them, and re-layouts  0.97 us (3%)
    pallas_call x1, Pallas kernels, scan_body(): pl.pallas_call(functools.partial(scan_kernel, pieces, local, width, modes...  33.9 us
    unnamed x1, local copies, waits for them, and re-layouts  0.97 us

commit v1 on v0

--- a/solution.py
+++ b/solution.py
@@ -124,7 +124,9 @@
         lax.dynamic_slice_in_dim(scale, first_channel, share, 0),
     )
     chan_skip = lax.dynamic_slice_in_dim(skip_gain, first_channel, share, 0)
-    streams = jnp.take(vocab_table, token_ids, axis=0)
+    entries = jnp.arange(vocab_table.shape[0], dtype=token_ids.dtype)
+    chosen = (token_ids[:, None] == entries[None, :]).astype(vocab_table.dtype)
+    streams = jnp.einsum("nv,vjc->njc", chosen, vocab_table, preferred_element_type=jnp.float32)
     padded = jnp.pad(streams, ((rim, 0), (0, 0), (0, 0)))
     mixed = short_conv(padded, chan_taps, length)
     query = mixed[:, 0]
@@ -139,7 +141,6 @@
 HALO = 8
 UNROLL = 8
 CUTS = 4
-SPLITS = 1
 MESH = pl.DeviceIdType.MESH
 
 
@@ -162,7 +163,7 @@
     return value
 
 
-def scan_kernel(
+def trade_kernel(
     pieces,
     local,
     width,
@@ -180,6 +181,8 @@
     residue_ref,
     skip_ref,
     load_sem,
+    other_ref,
+    rows_ref,
     hot_ref,
     x_ref,
     query_ref,
@@ -187,43 +190,157 @@
     end_ref,
     begin_ref,
     coef_ref,
+    seed_ref,
+    last_ref,
     turn_ref,
     send_ref,
     send_sem,
     recv_sem,
     own_sem,
+    trade_sem,
+    ids_sem,
+    state_sem,
 ):
     me = lax.axis_index("seq")
-    slots = pieces // SUB
-    steps = toggles(me, pieces)
-    share = skip_ref.shape[1]
-    vocab = tab_ref.shape[1]
-    blocks = share // LANES
+    group = lax.axis_index("groups")
+    share = 2 * LANES
+    quarter = pieces // 4
+    half = me // SUB
+    plane = me // quarter
+    inner = plane * (3 - plane) // 2
+    upper = inner * half
+    is_inner = inner == 1
+    is_outer = inner == 0
+    partner = me + inner * quarter * (1 - 2 * half)
+    vocab = tab_ref.shape[2]
     length = pieces * local
-    mine = pl.ds(pl.multiple_of(me * share, LANES), share)
-    loads = (
-        (all_tab_ref, tab_ref),
-        (all_taps_ref.at[:, :, mine], taps_ref),
-        (all_decay_ref.at[:, mine], decay_ref),
-        (all_residue_ref.at[:, mine], residue_ref),
-        (all_skip_ref.at[:, mine], skip_ref),
-    )
-    loads = [
-        pltpu.make_async_copy(source, target, load_sem.at[i])
-        for i, (source, target) in enumerate(loads)
-    ]
-    for load in loads:
-        load.start()
+    steps = toggles(me, SUB)
+
+    bases = (
+        me * share + inner * group * LANES,
+        me * share + LANES + inner * ((partner - me) * share + (group - 1) * LANES),
+    )
+    bases = [pl.multiple_of(base, LANES) for base in bases]
+    offset = pl.multiple_of(inner * group * LANES, LANES)
+
+    def loads(block):
+        mine = pl.ds(bases[block], LANES)
+        pairs = (
+            (all_taps_ref.at[:, :, mine], taps_ref.at[block]),
+            (all_decay_ref.at[:, mine], decay_ref.at[block]),
+            (all_residue_ref.at[:, mine], residue_ref.at[block]),
+            (all_skip_ref.at[:, mine], skip_ref.at[block]),
+        )
+        return [
+            pltpu.make_async_copy(source, target, load_sem.at[block, i])
+            for i, (source, target) in enumerate(pairs)
+        ]
+
+    near_table = pltpu.make_async_copy(
+        all_tab_ref.at[:, :, pl.ds(offset, LANES)], tab_ref.at[0], load_sem.at[0, 4]
+    )
+    far_table = pltpu.make_async_copy(
+        all_tab_ref.at[:, :, pl.ds(LANES, LANES)], tab_ref.at[1], load_sem.at[1, 4]
+    )
+    near_table.start()
+
+    @pl.when(is_outer)
+    def _():
+        far_table.start()
+
+    for block in range(2):
+        for load in loads(block):
+            load.start()
+
     barrier = pltpu.get_barrier_semaphore()
-    for mask in range(1, pieces):
-        peer = flip(me, steps, mask)
-        pl.semaphore_signal(barrier, inc=1, device_id={"seq": peer}, device_id_type=MESH)
+
+    def greet(seq, at):
+        pl.semaphore_signal(
+            barrier, inc=1, device_id={"groups": at, "seq": seq}, device_id_type=MESH
+        )
+
+    @pl.when(is_inner)
+    def _():
+        greet(partner, group)
+
+    for j in range(quarter):
+        for seq in (j, 3 * quarter + j):
+
+            @pl.when(me != seq)
+            def _():
+                greet(seq, group)
+
+        friend = quarter + quarter * half + j
+        greet(friend, 1 - group)
+
+        @pl.when(me != friend)
+        def _():
+            greet(friend, group)
+
+    def trade(j):
+        return pltpu.make_async_remote_copy(
+            src_ref=tab_ref.at[0, j],
+            dst_ref=tab_ref.at[1, j],
+            send_sem=trade_sem.at[0, j],
+            recv_sem=trade_sem.at[1, j],
+            device_id={"groups": group, "seq": partner},
+            device_id_type=MESH,
+        )
+
+    swap_ids = pltpu.make_async_remote_copy(
+        src_ref=ids_ref,
+        dst_ref=other_ref,
+        send_sem=ids_sem.at[0],
+        recv_sem=ids_sem.at[1],
+        device_id={"groups": 1 - group, "seq": me},
+        device_id_type=MESH,
+    )
+
+    def pass_state(block):
+        return pltpu.make_async_remote_copy(
+            src_ref=last_ref.at[block],
+            dst_ref=seed_ref.at[1 - block],
+            send_sem=state_sem.at[0, block],
+            recv_sem=state_sem.at[1, 1 - block],
+            device_id={"groups": group, "seq": partner},
+            device_id_type=MESH,
+        )
+
+    def earlier(ids):
+        first = lax.broadcasted_iota(jnp.int32, ids.shape, 0) == 0
+        return jnp.where(first, -1, pltpu.roll(ids, 1, axis=0))
+
+    near_table.wait()
+    ids = ids_ref[...]
+    before = earlier(ids)
+
+    @pl.when(is_outer)
+    def _():
+        rows_ref[0] = ids
+        rows_ref[1] = before
+        far_table.wait()
+
+    @pl.when(is_inner)
+    def _():
+        pl.semaphore_wait(barrier, pieces)
+        swap_ids.start()
+        for j in range(3):
+            trade(j).start()
+        swap_ids.wait_recv()
+        other = other_ref[...]
+        for i, pair in enumerate(((ids, other), (before, earlier(other)))):
+            for s in range(2):
+                rows_ref[i, s * SUB : (s + 1) * SUB, :] = jnp.where(
+                    half == 1, pair[s][SUB:, :], pair[s][:SUB, :]
+                )
+
+    @pl.when(upper == 0)
+    def _():
+        seed_ref[...] = jnp.zeros_like(seed_ref)
 
     cut = (HALO + local) * pieces // CUTS
-    ids = ids_ref[...]
-    before = jnp.where(
-        lax.broadcasted_iota(jnp.int32, ids.shape, 0) == 0, -1, pltpu.roll(ids, 1, axis=0)
-    )
+    ids = rows_ref[0]
+    before = rows_ref[1]
     entry = lax.broadcasted_iota(jnp.int32, (pieces, vocab), 1)
     count = (HALO + local) // CUTS
 
@@ -235,43 +352,48 @@
             ).astype(jnp.bfloat16)
 
     build(0)
-    for load in loads:
-        load.wait()
-
-    height = local // SPLITS
-
-    def place(block, part, source):
-        return out_ref.at[
-            pl.ds(part * height, height),
-            pl.ds(pl.multiple_of(source * share + block * LANES, LANES), LANES),
-        ]
-
-    def remote(block, part, mask, peer, source):
+    for block in range(2):
+        for load in loads(block):
+            load.wait()
+
+    def base_of(block):
+        return pl.multiple_of(bases[0] + block * (bases[1] - bases[0]), LANES)
+
+    def place(base):
+        return out_ref.at[:, pl.ds(base, LANES)]
+
+    def target(slot, low):
+        seq = (1 - inner) * (slot * SUB + low) + inner * (half * SUB + low)
+        return {"groups": group + inner * slot * (1 - 2 * group), "seq": seq}
+
+    def remote(block, slot, k):
+        low = flip(me, steps, k) - half * SUB
+        base = base_of(block)
         return pltpu.make_async_remote_copy(
-            src_ref=send_ref.at[block, peer, pl.ds(part * height, height)],
-            dst_ref=place(block, part, source),
-            send_sem=send_sem.at[block, part, mask],
-            recv_sem=recv_sem.at[block, part, mask],
-            device_id={"seq": peer},
+            src_ref=send_ref.at[block, slot * SUB + low],
+            dst_ref=place(base),
+            send_sem=send_sem.at[block, slot, k],
+            recv_sem=recv_sem.at[base // LANES],
+            device_id=target(slot, low),
             device_id_type=MESH,
         )
 
-    def own(block, part):
+    own_slot = (1 - inner) * half
+
+    def own(block):
         return pltpu.make_async_copy(
-            send_ref.at[block, me, pl.ds(part * height, height)],
-            place(block, part, me),
-            own_sem.at[block, part],
+            send_ref.at[block, own_slot * SUB + me - half * SUB],
+            place(base_of(block)),
+            own_sem.at[block],
         )
 
-    for block in range(blocks):
-        lane = pl.ds(block * LANES, LANES)
-        rate = decay_ref[:, lane] / length
+    def head(block):
+        rate = decay_ref[block] / length
         pole = jnp.exp(-rate)
-        leap = jnp.exp(-rate * local)
-        coef_ref[0] = pole
-        coef_ref[1] = residue_ref[:, lane] * jnp.sqrt(2.0 * rate)
-        skip = wide(skip_ref[:, lane])
-        table = jnp.concatenate([tab_ref[j, :, lane] for j in range(3)], axis=1)
+        coef_ref[block, 0] = pole
+        coef_ref[block, 1] = residue_ref[block] * jnp.sqrt(2.0 * rate)
+        coef_ref[block, 2] = jnp.exp(-rate * local)
+        table = jnp.concatenate([tab_ref[block, j] for j in range(3)], axis=1)
         for i in range(CUTS):
             if block == 0 and i + 1 < CUTS:
                 build(i + 1)
@@ -280,9 +402,10 @@
 
         def first_pass(slot, _):
             base = pl.multiple_of(slot * SUB, SUB)
-            poles = [wide(coef_ref[0, s : s + 1, :]) for s in range(modes)]
+            poles = [wide(coef_ref[block, 0, s : s + 1, :]) for s in range(modes)]
             taps = [
-                [wide(taps_ref[j, lag : lag + 1, lane]) for lag in range(width)] for j in range(3)
+                [wide(taps_ref[block, j, lag : lag + 1, :]) for lag in range(width)]
+                for j in range(3)
             ]
 
             def step(i, state):
@@ -303,8 +426,8 @@
                 for t in range(UNROLL):
                     at = pl.multiple_of((i * UNROLL + t) * pieces + base, SUB)
                     gated = mixed[1][t] * mixed[2][t]
-                    query_ref[pl.ds(at, SUB), :] = mixed[0][t]
-                    gated_ref[pl.ds(at, SUB), :] = gated
+                    query_ref[block, pl.ds(at, SUB), :] = mixed[0][t]
+                    gated_ref[block, pl.ds(at, SUB), :] = gated
                     for s in range(modes):
                         state[s] = poles[s] * state[s] + gated
                 return tuple(state)
@@ -312,26 +435,43 @@
             zero = jnp.zeros((SUB, LANES), jnp.float32)
             state = lax.fori_loop(0, local // UNROLL, step, (zero,) * modes)
             for s in range(modes):
-                end_ref[pl.ds(pl.multiple_of(s * pieces + base, SUB), SUB), :] = state[s]
+                end_ref[block, pl.ds(pl.multiple_of(s * pieces + base, SUB), SUB), :] = state[s]
             return 0
 
-        lax.fori_loop(0, slots, first_pass, 0)
-        carry = jnp.zeros((modes, LANES), jnp.float32)
+        lax.fori_loop(0, 2, first_pass, 0)
+
+    def tail(block):
+        @pl.when(upper == 1)
+        def _():
+            pass_state(1 - block).wait_recv()
+
+        leap = coef_ref[block, 2]
+        carry = seed_ref[block, 0]
         for k in range(pieces):
+            if k == SUB:
+                last_ref[block, 0] = carry
+                carry = jnp.where(is_inner, seed_ref[block, 1], carry)
             begin_ref[pl.ds(k, modes, stride=pieces), :] = carry
-            carry = leap * carry + end_ref[pl.ds(k, modes, stride=pieces), :]
-
-        for far in range(slots - 1, -1, -1):
-            first = flip(me // SUB * SUB, steps, far * SUB)
-            base = pl.multiple_of(first, SUB)
-            poles = [wide(coef_ref[0, s : s + 1, :]) for s in range(modes)]
-            coefs = [wide(coef_ref[1, s : s + 1, :]) for s in range(modes)]
+            carry = leap * carry + end_ref[block, pl.ds(k, modes, stride=pieces), :]
+        last_ref[block, 1] = carry
+
+        @pl.when(inner - upper == 1)
+        def _():
+            pass_state(block).start()
+
+        skip = wide(skip_ref[block])
+        lead = (1 - inner) * half
+        for q in range(2):
+            slot = q + lead * (1 - 2 * q)
+            base = pl.multiple_of(slot * SUB, SUB)
+            poles = [wide(coef_ref[block, 0, s : s + 1, :]) for s in range(modes)]
+            coefs = [wide(coef_ref[block, 1, s : s + 1, :]) for s in range(modes)]
 
             def step(i, state):
                 state = list(state)
                 for t in range(UNROLL):
                     at = pl.multiple_of((i * UNROLL + t) * pieces + base, SUB)
-                    gated = gated_ref[pl.ds(at, SUB), :]
+                    gated = gated_ref[block, pl.ds(at, SUB), :]
                     terms = [skip * gated]
                     for s in range(modes):
                         state[s] = poles[s] * state[s] + gated
@@ -342,7 +482,7 @@
                     for term in terms[1:]:
                         total = total + term
                     turn_ref[pl.ds(pl.multiple_of((i * UNROLL + t) * SUB, SUB), SUB), :] = (
-                        query_ref[pl.ds(at, SUB), :] * total
+                        query_ref[block, pl.ds(at, SUB), :] * total
                     )
                 return tuple(state)
 
@@ -350,77 +490,128 @@
                 begin_ref[pl.ds(pl.multiple_of(s * pieces + base, SUB), SUB), :]
                 for s in range(modes)
             )
-            for part in range(SPLITS):
-                low = part * height
-                state = lax.fori_loop(low // UNROLL, (low + height) // UNROLL, step, state)
-                for k in range(SUB):
-                    send_ref[block, first + k, low : low + height, :] = turn_ref[
-                        pl.ds(low * SUB + k, height, stride=SUB), :
-                    ].astype(jnp.bfloat16)
-                if block == 0 and far == slots - 1 and part == 0:
+            lax.fori_loop(0, local // UNROLL, step, state)
+            for k in range(SUB):
+                send_ref[block, base + k, :, :] = turn_ref[
+                    pl.ds(k, local, stride=SUB), :
+                ].astype(jnp.bfloat16)
+
+            if q == 0:
+
+                @pl.when(jnp.logical_and(is_outer, block == 0))
+                def _():
                     pl.semaphore_wait(barrier, pieces - 1)
-                for k in range(SUB):
-                    if far == 0 and k == 0:
-                        own(block, part).start()
-                    else:
-                        mask = far * SUB + k
-                        remote(block, part, mask, flip(me, steps, mask), me).start()
-
-    for block in range(blocks):
-        for part in range(SPLITS):
-            own(block, part).wait()
-            for mask in range(1, pieces):
-                peer = flip(me, steps, mask)
-                remote(block, part, mask, peer, me).wait_send()
-                remote(block, part, mask, me, peer).wait_recv()
-
-
-def scan_body(token_ids, vocab_table, short_filter, residue, decay, skip_gain):
+
+            for k in range(1, SUB):
+                remote(block, slot, k).start()
+
+            @pl.when(slot == own_slot)
+            def _():
+                own(block).start()
+
+            @pl.when(slot != own_slot)
+            def _():
+                remote(block, slot, 0).start()
+
+    head(0)
+    lax.fori_loop(0, 1 - upper, lambda i, _: (tail(0), 0)[1], 0)
+
+    @pl.when(is_inner)
+    def _():
+        for j in range(3):
+            trade(j).wait_recv()
+
+    head(1)
+    lax.fori_loop(0, 1 + upper, lambda i, _: (tail(1 - i), 0)[1], 0)
+
+    @pl.when(is_inner)
+    def _():
+        swap_ids.wait_send()
+        for j in range(3):
+            trade(j).wait_send()
+
+    @pl.when(inner - upper == 1)
+    def _():
+        for block in range(2):
+            pass_state(block).wait_send()
+
+    for block in range(2):
+        own(block).wait()
+        for slot in range(2):
+            for k in range(1, SUB):
+                remote(block, slot, k).wait_send()
+        remote(block, 1 - own_slot, 0).wait_send()
+
+    def arrive(at, _):
+        here = pl.multiple_of(at * LANES, LANES)
+
+        @pl.when(jnp.logical_and(here != bases[0], here != bases[1]))
+        def _():
+            pltpu.make_async_remote_copy(
+                src_ref=send_ref.at[0, 0],
+                dst_ref=place(here),
+                send_sem=send_sem.at[0, 0, 0],
+                recv_sem=recv_sem.at[at],
+                device_id={"groups": group, "seq": me},
+                device_id_type=MESH,
+            ).wait_recv()
+
+        return 0
+
+    lax.fori_loop(0, 2 * pieces, arrive, 0)
+
+
+def trade_body(token_ids, vocab_table, short_filter, residue, decay, skip_gain):
     pieces = lax.axis_size("seq")
     length = token_ids.shape[0]
     local = length // pieces
     vocab, streams, share = vocab_table.shape
     width = short_filter.shape[0]
     modes = decay.shape[1]
-    blocks = share // LANES
     ids = token_ids.reshape(pieces, local)
     table = vocab_table.transpose(1, 0, 2)
     taps = short_filter.transpose(1, 0, 2)
     rows = (HALO + local) * pieces
     vmem = pl.BlockSpec(memory_space=pltpu.VMEM)
     return pl.pallas_call(
-        functools.partial(scan_kernel, pieces, local, width, modes),
+        functools.partial(trade_kernel, pieces, local, width, modes),
         out_shape=pltpu.VMEM((local, pieces * share), jnp.bfloat16),
         in_specs=[vmem] + [pl.BlockSpec(memory_space=pl.ANY)] * 5,
         out_specs=pl.BlockSpec(memory_space=pltpu.VMEM),
         scratch_shapes=[
-            pltpu.VMEM((streams, vocab, share), vocab_table.dtype),
-            pltpu.VMEM((streams, width, share), jnp.float32),
-            pltpu.VMEM((modes, share), jnp.float32),
-            pltpu.VMEM((modes, share), jnp.float32),
-            pltpu.VMEM((1, share), jnp.float32),
-            pltpu.SemaphoreType.DMA((5,)),
+            pltpu.VMEM((2, streams, vocab, LANES), vocab_table.dtype),
+            pltpu.VMEM((2, streams, width, LANES), jnp.float32),
+            pltpu.VMEM((2, modes, LANES), jnp.float32),
+            pltpu.VMEM((2, modes, LANES), jnp.float32),
+            pltpu.VMEM((2, 1, LANES), jnp.float32),
+            pltpu.SemaphoreType.DMA((2, 5)),
+            pltpu.VMEM((pieces, local), jnp.int32),
+            pltpu.VMEM((2, pieces, local), jnp.int32),
             pltpu.VMEM((rows, vocab), jnp.bfloat16),
             pltpu.VMEM((rows, streams * LANES), jnp.float32),
-            pltpu.VMEM((length, LANES), jnp.float32),
-            pltpu.VMEM((length, LANES), jnp.float32),
+            pltpu.VMEM((2, length, LANES), jnp.float32),
+            pltpu.VMEM((2, length, LANES), jnp.float32),
+            pltpu.VMEM((2, modes * pieces, LANES), jnp.float32),
             pltpu.VMEM((modes * pieces, LANES), jnp.float32),
-            pltpu.VMEM((modes * pieces, LANES), jnp.float32),
-            pltpu.VMEM((2, modes, LANES), jnp.float32),
+            pltpu.VMEM((2, 3, modes, LANES), jnp.float32),
+            pltpu.VMEM((2, 2, modes, LANES), jnp.float32),
+            pltpu.VMEM((2, 2, modes, LANES), jnp.float32),
             pltpu.VMEM((local * SUB, LANES), jnp.float32),
-            pltpu.VMEM((blocks, pieces, local, LANES), jnp.bfloat16),
-            pltpu.SemaphoreType.DMA((blocks, SPLITS, pieces)),
-            pltpu.SemaphoreType.DMA((blocks, SPLITS, pieces)),
-            pltpu.SemaphoreType.DMA((blocks, SPLITS)),
+            pltpu.VMEM((2, pieces, local, LANES), jnp.bfloat16),
+            pltpu.SemaphoreType.DMA((2, 2, SUB)),
+            pltpu.SemaphoreType.DMA((2 * pieces,)),
+            pltpu.SemaphoreType.DMA((2,)),
+            pltpu.SemaphoreType.DMA((2, streams)),
+            pltpu.SemaphoreType.DMA((2,)),
+            pltpu.SemaphoreType.DMA((2, 2)),
         ],
         compiler_params=pltpu.CompilerParams(collective_id=0, has_side_effects=True),
     )(ids, table, taps, decay.T, residue.T, skip_gain[None])
 
 
-def fits(mesh, share, local, width):
-    pieces = mesh.shape["seq"]
-    even = pieces % (2 * SUB) == 0 and pieces & (pieces - 1) == 0
-    return share % LANES == 0 and even and local % (16 * SPLITS) == 0 and width <= HALO + 1
+def fits(mesh, share, local, width, streams):
+    even = mesh.shape["seq"] == 2 * SUB and mesh.shape["groups"] == 2
+    return even and share == 2 * LANES and local == LANES and width <= HALO + 1 and streams == 3
 
 
 def solution(mesh):
@@ -430,7 +621,8 @@
         pieces = mesh.shape["seq"]
         local = token_ids.shape[0] // (mesh.shape["groups"] * pieces)
         share = vocab_table.shape[2] // pieces
-        chosen = scan_body if fits(mesh, share, local, short_filter.shape[0]) else body
+        shapes = (share, local, short_filter.shape[0], vocab_table.shape[1])
+        chosen = trade_body if fits(mesh, *shapes) else body
         return jax.shard_map(
             chosen, mesh=mesh, in_specs=placed, out_specs=P(("groups", "seq"), None), check_vma=False
         )(token_ids, vocab_table, short_filter, residue, decay, skip_gain)

time: 35 us -> 38.6 us (1.10)
  the two profiles are of different devices: /device:TPU:9 before, /device:TPU:31 now
where the time goes in v1:
time: 38.6 us; the launch traced here: 38.4 us
  Pallas kernels  37.4 us (97%)
  local copies, waits for them, and re-layouts  0.97 us (3%)
    pallas_call x1, Pallas kernels, trade_body(): pl.pallas_call(functools.partial(trade_kernel, pieces, local, width, mode...  37.4 us
    unnamed x1, local copies, waits for them, and re-layouts  0.97 us

profile of v1, /device:TPU:31, one launch (start us, length us, event | category | flops | bytes accessed | tf_op | source)
XLA Modules:
  0.0 38.4 jit_solution(4769699353322933065)
XLA Ops:
  0.0 37.4 %shard_map.64 = bf16[128,4096]{1,0:T(8,128)(2,1)S(1)} custom-call(s32[16,128]{1,0:T(8,128)} %bitcast.11, bf16[3,512,256]{2,1,0:T(8,128)(2,1)} %bitcast.6, f32[3,7,4096]{2,1,0:T(8,128)} %bitcast.7, f32[16,4096]{1,0:T(8,128)} %bitcast.8, f32[16,4096]{1,0:T(8,128)} %bitcast.9, f32[1,4096]{1,0:T(1,128)} %bitcast.10), custom_call_target="tpu_custom_call" | custom-call | tf_op jit(solution)/shard_map/pallas_call | solution.py:576
  37.4 1.0 %copy.8 = bf16[128,4096]{1,0:T(8,128)(2,1)} copy(bf16[128,4096]{1,0:T(8,128)(2,1)S(1)} %shard_map.64) | data formatting | bytes 2097152

commit v2 on v0

v2 whole, which is shorter than its diff:
```python
import functools
import math

import jax
import jax.numpy as jnp
from jax import lax
from jax.experimental import pallas as pl
from jax.experimental.pallas import tpu as pltpu
from jax.sharding import PartitionSpec as P

HIGHEST = lax.Precision.HIGHEST


def angle_tables(first_index, second_index, modulus):
    product = first_index[:, None] * second_index[None, :] % modulus
    angle = product.astype(jnp.float32) * (2.0 * math.pi / modulus)
    return (jnp.cos(angle), jnp.sin(angle))


def short_conv(padded, taps, count):
    width = taps.shape[0]
    total = jnp.zeros((count,) + padded.shape[1:], jnp.float32)
    for lag in range(width):
        start = width - 1 - lag
        total = total + taps[lag] * padded[start : start + count].astype(jnp.float32)
    return total


def filter_spectrum(freq, total, pole, gap, tail, scale):
    theta = freq.astype(jnp.float32) * (2.0 * math.pi / total)
    sine = jnp.sin(theta)[:, :, None, None]
    halfsq = (jnp.sin(0.5 * theta) ** 2)[:, :, None, None]
    parity = (1 - 2 * (freq % 2)).astype(jnp.float32)[:, :, None, None]
    shape_out = freq.shape + (pole.shape[0],)
    real_part = jnp.zeros(shape_out, jnp.float32)
    imag_part = jnp.zeros(shape_out, jnp.float32)
    for first in range(0, pole.shape[1], 4):
        part_pole = pole[:, first : first + 4]
        dreal = gap[:, first : first + 4] + 2.0 * part_pole * halfsq
        dimag = part_pole * sine
        factor = (
            scale[:, first : first + 4]
            * (1.0 - tail[:, first : first + 4] * parity)
            / (dreal * dreal + dimag * dimag)
        )
        real_part = real_part + jnp.sum(factor * dreal, axis=-1)
        imag_part = imag_part - jnp.sum(factor * dimag, axis=-1)
    return (real_part, imag_part)


def convolve(gated, skip, filters, total, move_forward, move_back):
    pieces, block, width = gated.shape
    span = 2 * pieces
    outer_index = jnp.arange(span, dtype=jnp.int32)
    piece_index = jnp.arange(pieces, dtype=jnp.int32)
    outer_cos, outer_sin = angle_tables(outer_index, piece_index, span)
    real_part = jnp.einsum("kp,ptc->ktc", outer_cos, gated, precision=HIGHEST)
    imag_part = -jnp.einsum("kp,ptc->ktc", outer_sin, gated, precision=HIGHEST)
    times = jnp.arange(block, dtype=jnp.int32)
    twist_cos, twist_sin = angle_tables(outer_index, times, total)
    twist_cos = twist_cos[:, :, None]
    twist_sin = twist_sin[:, :, None]
    turned_real = twist_cos * real_part + twist_sin * imag_part
    turned_imag = twist_cos * imag_part - twist_sin * real_part
    moved = move_forward(jnp.stack([turned_real, turned_imag]))
    count = moved.shape[1]
    length = moved.shape[2]
    positions = jnp.arange(length, dtype=jnp.int32)
    inner_cos, inner_sin = angle_tables(positions, positions, length)
    freq_real = jnp.einsum("mt,ktc->kmc", inner_cos, moved[0], precision=HIGHEST) + jnp.einsum(
        "mt,ktc->kmc", inner_sin, moved[1], precision=HIGHEST
    )
    freq_imag = jnp.einsum("mt,ktc->kmc", inner_cos, moved[1], precision=HIGHEST) - jnp.einsum(
        "mt,ktc->kmc", inner_sin, moved[0], precision=HIGHEST
    )
    owned = jnp.arange(count, dtype=jnp.int32)
    freq = (owned[:, None] + span * positions[None, :]) % total
    filt_real, filt_imag = filter_spectrum(freq, total, *filters)
    prod_real = freq_real * filt_real - freq_imag * filt_imag
    prod_imag = freq_real * filt_imag + freq_imag * filt_real
    back_real = jnp.einsum("mt,kmc->ktc", inner_cos, prod_real, precision=HIGHEST) - jnp.einsum(
        "mt,kmc->ktc", inner_sin, prod_imag, precision=HIGHEST
    )
    back_imag = jnp.einsum("mt,kmc->ktc", inner_cos, prod_imag, precision=HIGHEST) + jnp.einsum(
        "mt,kmc->ktc", inner_sin, prod_real, precision=HIGHEST
    )
    undo_cos, undo_sin = angle_tables(owned, positions, total)
    undo_cos = undo_cos[:, :, None]
    undo_sin = undo_sin[:, :, None]
    untwist_real = undo_cos * back_real - undo_sin * back_imag
    untwist_imag = undo_cos * back_imag + undo_sin * back_real
    returned = move_back(jnp.stack([untwist_real, untwist_imag]))
    last_cos, last_sin = angle_tables(piece_index, outer_index, span)
    convolved = (
        jnp.einsum("pk,ktc->ptc", last_cos, returned[0], precision=HIGHEST)
        - jnp.einsum("pk,ktc->ptc", last_sin, returned[1], precision=HIGHEST)
    ) * (1.0 / total)
    return convolved + skip * gated


def unchanged(value):
    return value


def body(token_ids, vocab_table, short_filter, residue, decay, skip_gain):
    pieces = lax.axis_size("seq")
    place = lax.axis_index("seq")
    length = token_ids.shape[0]
    local = length // pieces
    share = vocab_table.shape[2]
    rim = short_filter.shape[0] - 1
    total = 2 * length
    rate = decay / length
    pole = jnp.exp(-rate)
    gap = -jnp.expm1(-rate)
    tail = jnp.exp(-decay)
    scale = residue * jnp.sqrt(2.0 * rate)
    first_channel = place * share
    chan_taps = lax.dynamic_slice_in_dim(short_filter, first_channel, share, 2)
    chan_filters = (
        lax.dynamic_slice_in_dim(pole, first_channel, share, 0),
        lax.dynamic_slice_in_dim(gap, first_channel, share, 0),
        lax.dynamic_slice_in_dim(tail, first_channel, share, 0),
        lax.dynamic_slice_in_dim(scale, first_channel, share, 0),
    )
    chan_skip = lax.dynamic_slice_in_dim(skip_gain, first_channel, share, 0)
    entries = jnp.arange(vocab_table.shape[0], dtype=token_ids.dtype)
    chosen = (token_ids[:, None] == entries[None, :]).astype(vocab_table.dtype)
    streams = jnp.einsum("nv,vjc->njc", chosen, vocab_table, preferred_element_type=jnp.float32)
    padded = jnp.pad(streams, ((rim, 0), (0, 0), (0, 0)))
    mixed = short_conv(padded, chan_taps, length)
    query = mixed[:, 0]
    gated = (mixed[:, 1] * mixed[:, 2]).reshape(pieces, local, share)
    convolved = convolve(gated, chan_skip, chan_filters, total, unchanged, unchanged)
    output = (query * convolved.reshape(length, share)).astype(jnp.bfloat16)
    return lax.all_to_all(output, "seq", split_axis=0, concat_axis=1, tiled=True)


LANES = 128
SUB = 8
HALO = 8
UNROLL = 8
CUTS = 2
MESH = pl.DeviceIdType.MESH


def wide(row):
    return jnp.broadcast_to(row, (SUB, LANES))


def toggles(value, limit):
    steps, bit = [], 1
    while bit < limit:
        steps.append((bit, bit - 2 * bit * (value // bit % 2)))
        bit = 2 * bit
    return steps


def flip(value, steps, mask):
    for bit, step in steps:
        if mask & bit:
            value = value + step
    return value


def scan_kernel(
    pieces,
    local,
    width,
    modes,
    all_ids_ref,
    all_tab_ref,
    all_taps_ref,
    all_decay_ref,
    all_residue_ref,
    all_skip_ref,
    out_ref,
    ids_ref,
    tab_ref,
    taps_ref,
    decay_ref,
    residue_ref,
    skip_ref,
    load_sem,
    ids_sem,
    hot_ref,
    x_ref,
    query_ref,
    gated_ref,
    end_ref,
    begin_ref,
    carry_ref,
    coef_ref,
    turn_ref,
    send_ref,
    send_sem,
    recv_sem,
    own_sem,
):
    me = lax.axis_index("seq")
    half = me // SUB
    share = 2 * LANES
    vocab = tab_ref.shape[2]
    length = pieces * local
    steps = toggles(me, SUB)

    def loads(block):
        mine = pl.ds(pl.multiple_of(me * share + block * LANES, LANES), LANES)
        lane = pl.ds(block * LANES, LANES)
        pairs = (
            (all_tab_ref.at[:, :, lane], tab_ref.at[block]),
            (all_taps_ref.at[:, :, mine], taps_ref.at[block]),
            (all_decay_ref.at[:, mine], decay_ref.at[block]),
            (all_residue_ref.at[:, mine], residue_ref.at[block]),
            (all_skip_ref.at[:, mine], skip_ref.at[block]),
        )
        return [
            pltpu.make_async_copy(source, target, load_sem.at[block, i])
            for i, (source, target) in enumerate(pairs)
        ]

    load_ids = pltpu.make_async_copy(all_ids_ref, ids_ref, ids_sem.at[0])
    load_ids.start()
    for block in range(2):
        for load in loads(block):
            load.start()
    barrier = pltpu.get_barrier_semaphore()

    def greet(i, _):
        peer = me + i - pieces * ((me + i) // pieces)
        pl.semaphore_signal(barrier, inc=1, device_id={"seq": peer}, device_id_type=MESH)
        return 0

    lax.fori_loop(1, pieces, greet, 0)

    load_ids.wait()
    ids = ids_ref[...]
    before = jnp.where(
        lax.broadcasted_iota(jnp.int32, ids.shape, 0) == 0, -1, pltpu.roll(ids, 1, axis=0)
    )
    entry = lax.broadcasted_iota(jnp.int32, (SUB, vocab), 1)

    count = (HALO + local) // CUTS

    def build(slot, i):
        rows = slice(slot * SUB, (slot + 1) * SUB)
        for t in range(i * count - HALO, (i + 1) * count - HALO, 2):
            pair = []
            for at in (t, t + 1):
                column = (
                    ids[rows, at : at + 1] if at >= 0 else before[rows, local + at : local + at + 1]
                )
                pair.append(jnp.where(column == entry, 1.0, 0.0))
            hot_ref[slot, (HALO + t) * SUB : (HALO + t + 2) * SUB, :] = jnp.concatenate(
                pair, axis=0
            ).astype(jnp.bfloat16)

    def place(block, source):
        return out_ref.at[
            :, pl.ds(pl.multiple_of(source * share + block * LANES, LANES), LANES)
        ]

    def remote(block, slot, low, sender):
        peer = slot * SUB + low
        return pltpu.make_async_remote_copy(
            src_ref=send_ref.at[block, peer],
            dst_ref=place(block, sender),
            send_sem=send_sem.at[block, peer],
            recv_sem=recv_sem.at[block, sender],
            device_id={"seq": peer},
            device_id_type=MESH,
        )

    def own(block):
        return pltpu.make_async_copy(send_ref.at[block, me], place(block, me), own_sem.at[block])

    cut = (HALO + local) * SUB // CUTS

    def head(block, slot):
        if block == 0:
            for i in range(CUTS if slot == 0 else 1):
                build(slot, i)
        if slot == 0:
            for load in loads(block):
                load.wait()
            rate = decay_ref[block] / length
            coef_ref[0] = jnp.exp(-rate)
            coef_ref[1] = residue_ref[block] * jnp.sqrt(2.0 * rate)
            coef_ref[2] = jnp.exp(-rate * local)
            carry_ref[...] = jnp.zeros_like(carry_ref)

        table = jnp.concatenate([tab_ref[block, j] for j in range(3)], axis=1)
        for i in range(CUTS):
            if block == 0 and slot == 1 and i + 1 < CUTS:
                build(slot, i + 1)
            span = pl.ds(i * cut, cut)
            x_ref[span, :] = jnp.dot(
                hot_ref[slot, span, :], table, preferred_element_type=jnp.float32
            )
        poles = [wide(coef_ref[0, s : s + 1, :]) for s in range(modes)]
        taps = [
            [wide(taps_ref[block, j, lag : lag + 1, :]) for lag in range(width)] for j in range(3)
        ]

        def step(i, state):
            state = list(state)
            mixed = []
            for j in range(3):
                seen = {}
                for t in range(1 - width, UNROLL):
                    at = pl.multiple_of((i * UNROLL + t + HALO) * SUB, SUB)
                    seen[t] = x_ref[pl.ds(at, SUB), j * LANES : (j + 1) * LANES]
                totals = []
                for t in range(UNROLL):
                    total = taps[j][0] * seen[t]
                    for lag in range(1, width):
                        total = total + taps[j][lag] * seen[t - lag]
                    totals.append(total)
                mixed.append(totals)
            for t in range(UNROLL):
                at = pl.multiple_of((i * UNROLL + t) * SUB, SUB)
                gated = mixed[1][t] * mixed[2][t]
                query_ref[slot, pl.ds(at, SUB), :] = mixed[0][t]
                gated_ref[slot, pl.ds(at, SUB), :] = gated
                for s in range(modes):
                    state[s] = poles[s] * state[s] + gated
            return tuple(state)

        zero = jnp.zeros((SUB, LANES), jnp.float32)
        state = lax.fori_loop(0, local // UNROLL, step, (zero,) * modes)
        for s in range(modes):
            end_ref[s * SUB : (s + 1) * SUB, :] = state[s]
        leap = coef_ref[2]
        carry = carry_ref[...]
        for k in range(SUB):
            begin_ref[slot, pl.ds(k, modes, stride=SUB), :] = carry
            carry = leap * carry + end_ref[pl.ds(k, modes, stride=SUB), :]
        carry_ref[...] = carry

    def tail(block, slot, first):
        poles = [wide(coef_ref[0, s : s + 1, :]) for s in range(modes)]
        coefs = [wide(coef_ref[1, s : s + 1, :]) for s in range(modes)]
        skip = wide(skip_ref[block])

        def step(i, state):
            state = list(state)
            for t in range(UNROLL):
                at = pl.multiple_of((i * UNROLL + t) * SUB, SUB)
                gated = gated_ref[slot, pl.ds(at, SUB), :]
                terms = [skip * gated]
                for s in range(modes):
                    state[s] = poles[s] * state[s] + gated
                    terms.append(coefs[s] * state[s])
                    if len(terms) == 5:
                        terms = [((terms[0] + terms[1]) + (terms[2] + terms[3])) + terms[4]]
                total = terms[0]
                for term in terms[1:]:
                    total = total + term
                turn_ref[pl.ds(at, SUB), :] = query_ref[slot, pl.ds(at, SUB), :] * total
            return tuple(state)

        state = tuple(begin_ref[slot, s * SUB : (s + 1) * SUB, :] for s in range(modes))
        lax.fori_loop(0, local // UNROLL, step, state)
        for k in range(SUB):
            send_ref[block, slot * SUB + k] = turn_ref[pl.ds(k, local, stride=SUB), :].astype(
                jnp.bfloat16
            )

        @pl.when(first)
        def _():
            pl.semaphore_wait(barrier, pieces - 1)

        for k in range(SUB):
            low = k

            @pl.when(slot * SUB + low != me)
            def _():
                remote(block, slot, low, me).start()

        @pl.when(slot == half)
        def _():
            own(block).start()

    for block in range(2):
        head(block, 0)

        def early(i, _):
            tail(block, 0, block == 0)
            return 0

        lax.fori_loop(0, half, early, 0)
        head(block, 1)

        def late(i, _):
            tail(block, 1 - i, jnp.logical_and(half + i == 0, block == 0))
            return 0

        lax.fori_loop(0, 2 - half, late, 0)

    for block in range(2):
        own(block).wait()

        def finish(i, _):
            peer = me + i - pieces * ((me + i) // pieces)
            remote(block, peer // SUB, peer - peer // SUB * SUB, me).wait_send()
            remote(block, half, me - half * SUB, peer).wait_recv()
            return 0

        lax.fori_loop(1, pieces, finish, 0)


def scan_body(token_ids, vocab_table, short_filter, residue, decay, skip_gain):
    pieces = lax.axis_size("seq")
    length = token_ids.shape[0]
    local = length // pieces
    vocab, streams, share = vocab_table.shape
    width = short_filter.shape[0]
    modes = decay.shape[1]
    ids = token_ids.reshape(pieces, local)
    table = vocab_table.transpose(1, 0, 2)
    taps = short_filter.transpose(1, 0, 2)
    rows = (HALO + local) * SUB
    return pl.pallas_call(
        functools.partial(scan_kernel, pieces, local, width, modes),
        out_shape=pltpu.VMEM((local, pieces * share), jnp.bfloat16),
        in_specs=[pl.BlockSpec(memory_space=pl.ANY)] * 6,
        out_specs=pl.BlockSpec(memory_space=pltpu.VMEM),
        scratch_shapes=[
            pltpu.VMEM((pieces, local), jnp.int32),
            pltpu.VMEM((2, streams, vocab, LANES), vocab_table.dtype),
            pltpu.VMEM((2, streams, width, LANES), jnp.float32),
            pltpu.VMEM((2, modes, LANES), jnp.float32),
            pltpu.VMEM((2, modes, LANES), jnp.float32),
            pltpu.VMEM((2, 1, LANES), jnp.float32),
            pltpu.SemaphoreType.DMA((2, 5)),
            pltpu.SemaphoreType.DMA((1,)),
            pltpu.VMEM((2, rows, vocab), jnp.bfloat16),
            pltpu.VMEM((rows, streams * LANES), jnp.float32),
            pltpu.VMEM((2, local * SUB, LANES), jnp.float32),
            pltpu.VMEM((2, local * SUB, LANES), jnp.float32),
            pltpu.VMEM((modes * SUB, LANES), jnp.float32),
            pltpu.VMEM((2, modes * SUB, LANES), jnp.float32),
            pltpu.VMEM((modes, LANES), jnp.float32),
            pltpu.VMEM((3, modes, LANES), jnp.float32),
            pltpu.VMEM((local * SUB, LANES), jnp.float32),
            pltpu.VMEM((2, pieces, local, LANES), jnp.bfloat16),
            pltpu.SemaphoreType.DMA((2, pieces)),
            pltpu.SemaphoreType.DMA((2, pieces)),
            pltpu.SemaphoreType.DMA((2,)),
        ],
        compiler_params=pltpu.CompilerParams(collective_id=0, has_side_effects=True),
    )(ids, table, taps, decay.T, residue.T, skip_gain[None])


def fits(mesh, share, local, width, streams):
    even = mesh.shape["seq"] == 2 * SUB
    return even and share == 2 * LANES and local == LANES and width <= HALO + 1 and streams == 3


def solution(mesh):
    placed = (P("groups"), P(None, None, "seq"), P(), P(), P(), P())

    def whole(token_ids, vocab_table, short_filter, residue, decay, skip_gain):
        pieces = mesh.shape["seq"]
        local = token_ids.shape[0] // (mesh.shape["groups"] * pieces)
        share = vocab_table.shape[2] // pieces
        shapes = (share, local, short_filter.shape[0], vocab_table.shape[1])
        chosen = scan_body if fits(mesh, *shapes) else body
        return jax.shard_map(
            chosen, mesh=mesh, in_specs=placed, out_specs=P(("groups", "seq"), None), check_vma=False
        )(token_ids, vocab_table, short_filter, residue, decay, skip_gain)

    return whole
```

time: 35 us -> 32.5 us (0.929)
  the two profiles are of different devices: /device:TPU:9 before, /device:TPU:31 now
where the time goes in v2:
time: 32.5 us; the launch traced here: 32.3 us
  Pallas kernels  31.3 us (96%)
  local copies, waits for them, and re-layouts  0.97 us (3%)
    pallas_call x1, Pallas kernels, scan_body(): pl.pallas_call(functools.partial(scan_kernel, pieces, local, width, modes...  31.3 us
    unnamed x1, local copies, waits for them, and re-layouts  0.97 us

profile of v2, /device:TPU:31, one launch (start us, length us, event | category | flops | bytes accessed | tf_op | source)
XLA Modules:
  0.0 32.3 jit_solution(7689853027722379888)
XLA Ops:
  0.0 31.3 %shard_map.64 = bf16[128,4096]{1,0:T(8,128)(2,1)S(1)} custom-call(s32[16,128]{1,0:T(8,128)} %bitcast.11, bf16[3,512,256]{2,1,0:T(8,128)(2,1)} %bitcast.6, f32[3,7,4096]{2,1,0:T(8,128)} %bitcast.7, f32[16,4096]{1,0:T(8,128)} %bitcast.8, f32[16,4096]{1,0:T(8,128)} %bitcast.9, f32[1,4096]{1,0:T(1,128)} %bitcast.10), custom_call_target="tpu_custom_call" | custom-call | tf_op jit(solution)/shard_map/pallas_call | solution.py:423
  31.3 1.0 %copy.8 = bf16[128,4096]{1,0:T(8,128)(2,1)} copy(bf16[128,4096]{1,0:T(8,128)(2,1)S(1)} %shard_map.64) | data formatting | bytes 2097152

commit v3 on v2

--- a/solution.py
+++ b/solution.py
@@ -140,7 +140,8 @@
 SUB = 8
 HALO = 8
 UNROLL = 8
-CUTS = 2
+CUTS = 4
+PARTS = 8
 MESH = pl.DeviceIdType.MESH
 
 
@@ -238,9 +239,11 @@
     before = jnp.where(
         lax.broadcasted_iota(jnp.int32, ids.shape, 0) == 0, -1, pltpu.roll(ids, 1, axis=0)
     )
-    entry = lax.broadcasted_iota(jnp.int32, (SUB, vocab), 1)
+    entry = lax.broadcasted_iota(jnp.int16, (2 * SUB, vocab), 1)
 
     count = (HALO + local) // CUTS
+    one = jnp.ones(entry.shape, jnp.bfloat16)
+    nought = jnp.zeros(entry.shape, jnp.bfloat16)
 
     def build(slot, i):
         rows = slice(slot * SUB, (slot + 1) * SUB)
@@ -250,36 +253,57 @@
                 column = (
                     ids[rows, at : at + 1] if at >= 0 else before[rows, local + at : local + at + 1]
                 )
-                pair.append(jnp.where(column == entry, 1.0, 0.0))
-            hot_ref[slot, (HALO + t) * SUB : (HALO + t + 2) * SUB, :] = jnp.concatenate(
-                pair, axis=0
-            ).astype(jnp.bfloat16)
-
-    def place(block, source):
+                pair.append(jnp.broadcast_to(column, (SUB, LANES)))
+            pair = jnp.concatenate(pair, axis=0).astype(jnp.int16)
+            pair = jnp.concatenate([pair] * (vocab // LANES), axis=1)
+            hot_ref[slot, (HALO + t) * SUB : (HALO + t + 2) * SUB, :] = jnp.where(
+                pair == entry, one, nought
+            )
+
+    everything = pl.ds(0, local)
+
+    def place(block, source, span):
         return out_ref.at[
-            :, pl.ds(pl.multiple_of(source * share + block * LANES, LANES), LANES)
+            span, pl.ds(pl.multiple_of(source * share + block * LANES, LANES), LANES)
         ]
 
-    def remote(block, slot, low, sender):
+    def remote(block, slot, low, sender, span=everything):
         peer = slot * SUB + low
         return pltpu.make_async_remote_copy(
-            src_ref=send_ref.at[block, peer],
-            dst_ref=place(block, sender),
+            src_ref=send_ref.at[block, peer, span],
+            dst_ref=place(block, sender, span),
             send_sem=send_sem.at[block, peer],
             recv_sem=recv_sem.at[block, sender],
             device_id={"seq": peer},
             device_id_type=MESH,
         )
 
-    def own(block):
-        return pltpu.make_async_copy(send_ref.at[block, me], place(block, me), own_sem.at[block])
+    def own(block, span=everything):
+        return pltpu.make_async_copy(
+            send_ref.at[block, me, span], place(block, me, span), own_sem.at[block]
+        )
 
     cut = (HALO + local) * SUB // CUTS
+
+    def taps_of(block, j):
+        return [wide(taps_ref[block, j, lag : lag + 1, :]) for lag in range(width)]
+
+    def mix(rows_ref, taps, i):
+        seen = {}
+        for t in range(1 - width, UNROLL):
+            at = pl.multiple_of((i * UNROLL + t + HALO) * SUB, SUB)
+            seen[t] = rows_ref[pl.ds(at, SUB), :]
+        totals = []
+        for t in range(UNROLL):
+            total = taps[0] * seen[t]
+            for lag in range(1, width):
+                total = total + taps[lag] * seen[t - lag]
+            totals.append(total)
+        return totals
 
     def head(block, slot):
         if block == 0:
-            for i in range(CUTS if slot == 0 else 1):
-                build(slot, i)
+            build(slot, 0)
         if slot == 0:
             for load in loads(block):
                 load.wait()
@@ -289,38 +313,25 @@
             coef_ref[2] = jnp.exp(-rate * local)
             carry_ref[...] = jnp.zeros_like(carry_ref)
 
-        table = jnp.concatenate([tab_ref[block, j] for j in range(3)], axis=1)
+        table = jnp.concatenate([tab_ref[block, j] for j in (1, 2)], axis=1)
         for i in range(CUTS):
-            if block == 0 and slot == 1 and i + 1 < CUTS:
+            if block == 0 and i + 1 < CUTS:
                 build(slot, i + 1)
             span = pl.ds(i * cut, cut)
             x_ref[span, :] = jnp.dot(
                 hot_ref[slot, span, :], table, preferred_element_type=jnp.float32
             )
         poles = [wide(coef_ref[0, s : s + 1, :]) for s in range(modes)]
-        taps = [
-            [wide(taps_ref[block, j, lag : lag + 1, :]) for lag in range(width)] for j in range(3)
-        ]
+        taps = [taps_of(block, j) for j in (1, 2)]
 
         def step(i, state):
             state = list(state)
-            mixed = []
-            for j in range(3):
-                seen = {}
-                for t in range(1 - width, UNROLL):
-                    at = pl.multiple_of((i * UNROLL + t + HALO) * SUB, SUB)
-                    seen[t] = x_ref[pl.ds(at, SUB), j * LANES : (j + 1) * LANES]
-                totals = []
-                for t in range(UNROLL):
-                    total = taps[j][0] * seen[t]
-                    for lag in range(1, width):
-                        total = total + taps[j][lag] * seen[t - lag]
-                    totals.append(total)
-                mixed.append(totals)
+            mixed = [
+                mix(x_ref.at[:, j * LANES : (j + 1) * LANES], taps[j], i) for j in range(2)
+            ]
             for t in range(UNROLL):
                 at = pl.multiple_of((i * UNROLL + t) * SUB, SUB)
-                gated = mixed[1][t] * mixed[2][t]
-                query_ref[slot, pl.ds(at, SUB), :] = mixed[0][t]
+                gated = mixed[0][t] * mixed[1][t]
                 gated_ref[slot, pl.ds(at, SUB), :] = gated
                 for s in range(modes):
                     state[s] = poles[s] * state[s] + gated
@@ -341,9 +352,14 @@
         poles = [wide(coef_ref[0, s : s + 1, :]) for s in range(modes)]
         coefs = [wide(coef_ref[1, s : s + 1, :]) for s in range(modes)]
         skip = wide(skip_ref[block])
+        taps = taps_of(block, 0)
+        query_ref[...] = jnp.dot(
+            hot_ref[slot], tab_ref[block, 0], preferred_element_type=jnp.float32
+        )
 
         def step(i, state):
             state = list(state)
+            query = mix(query_ref, taps, i)
             for t in range(UNROLL):
                 at = pl.multiple_of((i * UNROLL + t) * SUB, SUB)
                 gated = gated_ref[slot, pl.ds(at, SUB), :]
@@ -356,30 +372,37 @@
                 total = terms[0]
                 for term in terms[1:]:
                     total = total + term
-                turn_ref[pl.ds(at, SUB), :] = query_ref[slot, pl.ds(at, SUB), :] * total
+                turn_ref[pl.ds(at, SUB), :] = query[t] * total
             return tuple(state)
 
         state = tuple(begin_ref[slot, s * SUB : (s + 1) * SUB, :] for s in range(modes))
-        lax.fori_loop(0, local // UNROLL, step, state)
-        for k in range(SUB):
-            send_ref[block, slot * SUB + k] = turn_ref[pl.ds(k, local, stride=SUB), :].astype(
-                jnp.bfloat16
+        parts = PARTS if block == 0 else 1
+        height = local // parts
+        for part in range(parts):
+            span = pl.ds(part * height, height)
+            state = lax.fori_loop(
+                part * height // UNROLL, (part + 1) * height // UNROLL, step, state
             )
-
-        @pl.when(first)
-        def _():
-            pl.semaphore_wait(barrier, pieces - 1)
-
-        for k in range(SUB):
-            low = k
-
-            @pl.when(slot * SUB + low != me)
+            for k in range(SUB):
+                send_ref[block, slot * SUB + k, span, :] = turn_ref[
+                    pl.ds(part * height * SUB + k, height, stride=SUB), :
+                ].astype(jnp.bfloat16)
+
+            if part == 0:
+
+                @pl.when(first)
+                def _():
+                    pl.semaphore_wait(barrier, pieces - 1)
+
+            for low in range(SUB):
+
+                @pl.when(slot * SUB + low != me)
+                def _():
+                    remote(block, slot, low, me, span).start()
+
+            @pl.when(slot == half)
             def _():
-                remote(block, slot, low, me).start()
-
-        @pl.when(slot == half)
-        def _():
-            own(block).start()
+                own(block, span).start()
 
     for block in range(2):
         head(block, 0)
@@ -435,8 +458,8 @@
             pltpu.SemaphoreType.DMA((2, 5)),
             pltpu.SemaphoreType.DMA((1,)),
             pltpu.VMEM((2, rows, vocab), jnp.bfloat16),
-            pltpu.VMEM((rows, streams * LANES), jnp.float32),
-            pltpu.VMEM((2, local * SUB, LANES), jnp.float32),
+            pltpu.VMEM((rows, 2 * LANES), jnp.float32),
+            pltpu.VMEM((rows, LANES), jnp.float32),
             pltpu.VMEM((2, local * SUB, LANES), jnp.float32),
             pltpu.VMEM((modes * SUB, LANES), jnp.float32),
             pltpu.VMEM((2, modes * SUB, LANES), jnp.float32),

time: 32.5 us -> 30.9 us (0.951)
  Pallas kernels: 31.3 us -> 29.8 us
    pallas_call x1, Pallas kernels: 31.3 us -> 29.8 us  [scan_body(): pl.pallas_call(functools.partial(scan_kernel, pieces, local, width, modes...]
where the time goes in v3:
time: 30.9 us; the launch traced here: 30.7 us
  Pallas kernels  29.8 us (96%)
  local copies, waits for them, and re-layouts  0.97 us (3%)
    pallas_call x1, Pallas kernels, scan_body(): pl.pallas_call(functools.partial(scan_kernel, pieces, local, width, modes...  29.8 us
    unnamed x1, local copies, waits for them, and re-layouts  0.97 us

profile of v3, /device:TPU:31, one launch (start us, length us, event | category | flops | bytes accessed | tf_op | source)
XLA Modules:
  0.0 30.7 jit_solution(12005822112899151125)
XLA Ops:
  0.0 29.8 %shard_map.64 = bf16[128,4096]{1,0:T(8,128)(2,1)S(1)} custom-call(s32[16,128]{1,0:T(8,128)} %bitcast.11, bf16[3,512,256]{2,1,0:T(8,128)(2,1)} %bitcast.6, f32[3,7,4096]{2,1,0:T(8,128)} %bitcast.7, f32[16,4096]{1,0:T(8,128)} %bitcast.8, f32[16,4096]{1,0:T(8,128)} %bitcast.9, f32[1,4096]{1,0:T(1,128)} %bitcast.10), custom_call_target="tpu_custom_call" | custom-call | tf_op jit(solution)/shard_map/pallas_call | solution.py:446
  29.8 1.0 %copy.8 = bf16[128,4096]{1,0:T(8,128)(2,1)} copy(bf16[128,4096]{1,0:T(8,128)(2,1)S(1)} %shard_map.64) | data formatting | bytes 2097152

commit v4 on v3

--- a/solution.py
+++ b/solution.py
@@ -139,9 +139,10 @@
 LANES = 128
 SUB = 8
 HALO = 8
-UNROLL = 8
+LONG = 32
+UNROLL = 16
 CUTS = 4
-PARTS = 8
+FAR = (16, 32, 80,)
 MESH = pl.DeviceIdType.MESH
 
 
@@ -288,13 +289,13 @@
     def taps_of(block, j):
         return [wide(taps_ref[block, j, lag : lag + 1, :]) for lag in range(width)]
 
-    def mix(rows_ref, taps, i):
+    def mix(rows_ref, taps, i, unroll):
         seen = {}
-        for t in range(1 - width, UNROLL):
-            at = pl.multiple_of((i * UNROLL + t + HALO) * SUB, SUB)
+        for t in range(1 - width, unroll):
+            at = pl.multiple_of((i * unroll + t + HALO) * SUB, SUB)
             seen[t] = rows_ref[pl.ds(at, SUB), :]
         totals = []
-        for t in range(UNROLL):
+        for t in range(unroll):
             total = taps[0] * seen[t]
             for lag in range(1, width):
                 total = total + taps[lag] * seen[t - lag]
@@ -327,10 +328,10 @@
         def step(i, state):
             state = list(state)
             mixed = [
-                mix(x_ref.at[:, j * LANES : (j + 1) * LANES], taps[j], i) for j in range(2)
+                mix(x_ref.at[:, j * LANES : (j + 1) * LANES], taps[j], i, LONG) for j in range(2)
             ]
-            for t in range(UNROLL):
-                at = pl.multiple_of((i * UNROLL + t) * SUB, SUB)
+            for t in range(LONG):
+                at = pl.multiple_of((i * LONG + t) * SUB, SUB)
                 gated = mixed[0][t] * mixed[1][t]
                 gated_ref[slot, pl.ds(at, SUB), :] = gated
                 for s in range(modes):
@@ -338,7 +339,7 @@
             return tuple(state)
 
         zero = jnp.zeros((SUB, LANES), jnp.float32)
-        state = lax.fori_loop(0, local // UNROLL, step, (zero,) * modes)
+        state = lax.fori_loop(0, local // LONG, step, (zero,) * modes)
         for s in range(modes):
             end_ref[s * SUB : (s + 1) * SUB, :] = state[s]
         leap = coef_ref[2]
@@ -348,7 +349,7 @@
             carry = leap * carry + end_ref[pl.ds(k, modes, stride=SUB), :]
         carry_ref[...] = carry
 
-    def tail(block, slot, first):
+    def tail(block, slot, first, heights):
         poles = [wide(coef_ref[0, s : s + 1, :]) for s in range(modes)]
         coefs = [wide(coef_ref[1, s : s + 1, :]) for s in range(modes)]
         skip = wide(skip_ref[block])
@@ -359,7 +360,7 @@
 
         def step(i, state):
             state = list(state)
-            query = mix(query_ref, taps, i)
+            query = mix(query_ref, taps, i, UNROLL)
             for t in range(UNROLL):
                 at = pl.multiple_of((i * UNROLL + t) * SUB, SUB)
                 gated = gated_ref[slot, pl.ds(at, SUB), :]
@@ -376,23 +377,18 @@
             return tuple(state)
 
         state = tuple(begin_ref[slot, s * SUB : (s + 1) * SUB, :] for s in range(modes))
-        parts = PARTS if block == 0 else 1
-        height = local // parts
-        for part in range(parts):
-            span = pl.ds(part * height, height)
-            state = lax.fori_loop(
-                part * height // UNROLL, (part + 1) * height // UNROLL, step, state
-            )
+        low_end = 0
+        for part, height in enumerate(heights):
+            start, low_end = low_end, low_end + height
+            span = pl.ds(start, height)
+            state = lax.fori_loop(start // UNROLL, low_end // UNROLL, step, state)
             for k in range(SUB):
                 send_ref[block, slot * SUB + k, span, :] = turn_ref[
-                    pl.ds(part * height * SUB + k, height, stride=SUB), :
+                    pl.ds(start * SUB + k, height, stride=SUB), :
                 ].astype(jnp.bfloat16)
 
-            if part == 0:
-
-                @pl.when(first)
-                def _():
-                    pl.semaphore_wait(barrier, pieces - 1)
+            if first and part == 0:
+                pl.semaphore_wait(barrier, pieces - 1)
 
             for low in range(SUB):
 
@@ -406,19 +402,26 @@
 
     for block in range(2):
         head(block, 0)
+        far = FAR if block == 0 else (local,)
 
         def early(i, _):
-            tail(block, 0, block == 0)
+            tail(block, 0, block == 0, far)
             return 0
 
         lax.fori_loop(0, half, early, 0)
         head(block, 1)
 
-        def late(i, _):
-            tail(block, 1 - i, jnp.logical_and(half + i == 0, block == 0))
+        def far_late(i, _):
+            tail(block, 1, block == 0, far)
             return 0
 
-        lax.fori_loop(0, 2 - half, late, 0)
+        lax.fori_loop(0, 1 - half, far_late, 0)
+
+        def near_late(i, _):
+            tail(block, half, False, (local,))
+            return 0
+
+        lax.fori_loop(0, 1, near_late, 0)
 
     for block in range(2):
         own(block).wait()

time: 30.9 us -> 30.1 us (0.974)
  Pallas kernels: 29.8 us -> 29 us
    pallas_call x1, Pallas kernels: 29.8 us -> 29 us  [scan_body(): pl.pallas_call(functools.partial(scan_kernel, pieces, local, width, modes...]
where the time goes in v4:
time: 30.1 us; the launch traced here: 29.9 us
  Pallas kernels  29 us (96%)
  local copies, waits for them, and re-layouts  0.97 us (3%)
    pallas_call x1, Pallas kernels, scan_body(): pl.pallas_call(functools.partial(scan_kernel, pieces, local, width, modes...  29 us
    unnamed x1, local copies, waits for them, and re-layouts  0.97 us

profile of v4, /device:TPU:31, one launch (start us, length us, event | category | flops | bytes accessed | tf_op | source)
XLA Modules:
  0.0 29.9 jit_solution(16959125240666634681)
XLA Ops:
  0.0 29.0 %shard_map.64 = bf16[128,4096]{1,0:T(8,128)(2,1)S(1)} custom-call(s32[16,128]{1,0:T(8,128)} %bitcast.11, bf16[3,512,256]{2,1,0:T(8,128)(2,1)} %bitcast.6, f32[3,7,4096]{2,1,0:T(8,128)} %bitcast.7, f32[16,4096]{1,0:T(8,128)} %bitcast.8, f32[16,4096]{1,0:T(8,128)} %bitcast.9, f32[1,4096]{1,0:T(1,128)} %bitcast.10), custom_call_target="tpu_custom_call" | custom-call | tf_op jit(solution)/shard_map/pallas_call | solution.py:449
  29.0 1.0 %copy.8 = bf16[128,4096]{1,0:T(8,128)(2,1)} copy(bf16[128,4096]{1,0:T(8,128)(2,1)S(1)} %shard_map.64) | data formatting | bytes 2097152

commit v5 on v4

--- a/solution.py
+++ b/solution.py
@@ -140,6 +140,8 @@
 SUB = 8
 HALO = 8
 LONG = 32
+FIRST = (0, 1, 2, 3, 4, 5, 6, 7)
+SECOND = (0, 4, 1, 5, 2, 6, 3, 7)
 UNROLL = 16
 CUTS = 4
 FAR = (16, 32, 80,)
@@ -148,21 +150,6 @@
 
 def wide(row):
     return jnp.broadcast_to(row, (SUB, LANES))
-
-
-def toggles(value, limit):
-    steps, bit = [], 1
-    while bit < limit:
-        steps.append((bit, bit - 2 * bit * (value // bit % 2)))
-        bit = 2 * bit
-    return steps
-
-
-def flip(value, steps, mask):
-    for bit, step in steps:
-        if mask & bit:
-            value = value + step
-    return value
 
 
 def scan_kernel(
@@ -204,21 +191,22 @@
     share = 2 * LANES
     vocab = tab_ref.shape[2]
     length = pieces * local
-    steps = toggles(me, SUB)
-
-    def loads(block):
+
+    def loads(block, picked=range(7)):
         mine = pl.ds(pl.multiple_of(me * share + block * LANES, LANES), LANES)
         lane = pl.ds(block * LANES, LANES)
         pairs = (
-            (all_tab_ref.at[:, :, lane], tab_ref.at[block]),
+            (all_tab_ref.at[1, :, lane], tab_ref.at[block, 1]),
+            (all_tab_ref.at[2, :, lane], tab_ref.at[block, 2]),
             (all_taps_ref.at[:, :, mine], taps_ref.at[block]),
             (all_decay_ref.at[:, mine], decay_ref.at[block]),
             (all_residue_ref.at[:, mine], residue_ref.at[block]),
             (all_skip_ref.at[:, mine], skip_ref.at[block]),
+            (all_tab_ref.at[0, :, lane], tab_ref.at[block, 0]),
         )
         return [
-            pltpu.make_async_copy(source, target, load_sem.at[block, i])
-            for i, (source, target) in enumerate(pairs)
+            pltpu.make_async_copy(*pairs[i], load_sem.at[block, i])
+            for i in picked
         ]
 
     load_ids = pltpu.make_async_copy(all_ids_ref, ids_ref, ids_sem.at[0])
@@ -306,7 +294,7 @@
         if block == 0:
             build(slot, 0)
         if slot == 0:
-            for load in loads(block):
+            for load in loads(block, range(6)):
                 load.wait()
             rate = decay_ref[block] / length
             coef_ref[0] = jnp.exp(-rate)
@@ -348,6 +336,9 @@
             begin_ref[slot, pl.ds(k, modes, stride=SUB), :] = carry
             carry = leap * carry + end_ref[pl.ds(k, modes, stride=SUB), :]
         carry_ref[...] = carry
+        if slot == 0:
+            for load in loads(block, range(6, 7)):
+                load.wait()
 
     def tail(block, slot, first, heights):
         poles = [wide(coef_ref[0, s : s + 1, :]) for s in range(modes)]
@@ -390,7 +381,9 @@
             if first and part == 0:
                 pl.semaphore_wait(barrier, pieces - 1)
 
-            for low in range(SUB):
+            order = FIRST if block == 0 else SECOND
+            for k in range(SUB):
+                low = k + slot * (order[k] - k)
 
                 @pl.when(slot * SUB + low != me)
                 def _():
@@ -458,7 +451,7 @@
             pltpu.VMEM((2, modes, LANES), jnp.float32),
             pltpu.VMEM((2, modes, LANES), jnp.float32),
             pltpu.VMEM((2, 1, LANES), jnp.float32),
-            pltpu.SemaphoreType.DMA((2, 5)),
+            pltpu.SemaphoreType.DMA((2, 7)),
             pltpu.SemaphoreType.DMA((1,)),
             pltpu.VMEM((2, rows, vocab), jnp.bfloat16),
             pltpu.VMEM((rows, 2 * LANES), jnp.float32),

time: 30.1 us -> 30.1 us (level)
  no operation moved by 1% of the time
where the time goes in v5:
time: 30.1 us; the launch traced here: 29.9 us
  Pallas kernels  29 us (96%)
  local copies, waits for them, and re-layouts  0.97 us (3%)
    pallas_call x1, Pallas kernels, scan_body(): pl.pallas_call(functools.partial(scan_kernel, pieces, local, width, modes...  29 us
    unnamed x1, local copies, waits for them, and re-layouts  0.97 us

profile of v5, /device:TPU:31, one launch (start us, length us, event | category | flops | bytes accessed | tf_op | source)
XLA Modules:
  0.0 29.9 jit_solution(3422694981094400952)
XLA Ops:
  0.0 29.0 %shard_map.64 = bf16[128,4096]{1,0:T(8,128)(2,1)S(1)} custom-call(s32[16,128]{1,0:T(8,128)} %bitcast.11, bf16[3,512,256]{2,1,0:T(8,128)(2,1)} %bitcast.6, f32[3,7,4096]{2,1,0:T(8,128)} %bitcast.7, f32[16,4096]{1,0:T(8,128)} %bitcast.8, f32[16,4096]{1,0:T(8,128)} %bitcast.9, f32[1,4096]{1,0:T(1,128)} %bitcast.10), custom_call_target="tpu_custom_call" | custom-call | tf_op jit(solution)/shard_map/pallas_call | solution.py:442
  29.0 1.0 %copy.8 = bf16[128,4096]{1,0:T(8,128)(2,1)} copy(bf16[128,4096]{1,0:T(8,128)(2,1)S(1)} %shard_map.64) | data formatting | bytes 2097152

commit v6 on v5

--- a/solution.py
+++ b/solution.py
@@ -292,7 +292,10 @@
 
     def head(block, slot):
         if block == 0:
-            build(slot, 0)
+            if slot == 0:
+                build(0, 0)
+                build(1, 0)
+                build(1, 1)
         if slot == 0:
             for load in loads(block, range(6)):
                 load.wait()
@@ -304,7 +307,7 @@
 
         table = jnp.concatenate([tab_ref[block, j] for j in (1, 2)], axis=1)
         for i in range(CUTS):
-            if block == 0 and i + 1 < CUTS:
+            if block == 0 and i + 1 < CUTS and (slot, i) != (1, 0):
                 build(slot, i + 1)
             span = pl.ds(i * cut, cut)
             x_ref[span, :] = jnp.dot(

time: 30.1 us -> 30.1 us (level)
  no operation moved by 1% of the time
where the time goes in v6:
time: 30.1 us; the launch traced here: 29.9 us
  Pallas kernels  28.9 us (96%)
  local copies, waits for them, and re-layouts  0.97 us (3%)
    pallas_call x1, Pallas kernels, scan_body(): pl.pallas_call(functools.partial(scan_kernel, pieces, local, width, modes...  28.9 us
    unnamed x1, local copies, waits for them, and re-layouts  0.97 us

profile of v6, /device:TPU:31, one launch (start us, length us, event | category | flops | bytes accessed | tf_op | source)
XLA Modules:
  0.0 29.9 jit_solution(3559438717771439362)
XLA Ops:
  0.0 28.9 %shard_map.64 = bf16[128,4096]{1,0:T(8,128)(2,1)S(1)} custom-call(s32[16,128]{1,0:T(8,128)} %bitcast.11, bf16[3,512,256]{2,1,0:T(8,128)(2,1)} %bitcast.6, f32[3,7,4096]{2,1,0:T(8,128)} %bitcast.7, f32[16,4096]{1,0:T(8,128)} %bitcast.8, f32[16,4096]{1,0:T(8,128)} %bitcast.9, f32[1,4096]{1,0:T(1,128)} %bitcast.10), custom_call_target="tpu_custom_call" | custom-call | tf_op jit(solution)/shard_map/pallas_call | solution.py:445
  28.9 1.0 %copy.8 = bf16[128,4096]{1,0:T(8,128)(2,1)} copy(bf16[128,4096]{1,0:T(8,128)(2,1)S(1)} %shard_map.64) | data formatting | bytes 2097152
